TPU v7x, 256 devices: a whole 4x4x8 slice. The times are simulated.
256 devices in a mesh: expert: 32 (over y, z), unit: 8 (over x, core).
Axes of the slice: x: 4, y: 4, z: 8, core: 2. Of those that a mesh axis runs over, the one named last changes fastest.
Arguments:
- w_up: bfloat16 [128, 1536, 4096], P('expert', 'unit'), may hold values from -0.09375 to 0.09375
- cluster: int32 [128, 1], replicated, may hold values from 0 to 31
- counts: int32 [128], replicated, may hold values from 16 to 127
Outputs:
- merged: bfloat16 [32, 1536, 4096], P('expert', None, 'unit')
Inputs may be any that keep to these rules, and one draw needn't show every extreme that they name: Every cluster has at least one member.
All inputs are finite; a program needn't handle non-finite values.
Results may differ from a plain program's by a relative error of at most 0.0051.
Values may be sent and summed in bfloat16 or wider, within the bound.
No kernel may reach another device: no remote copies, remote signals or barrier semaphores. Data moves between devices by JAX's collectives and lax.ppermute only.
A program may use at most 128 MiB of HBM per device.

v0:
```python
import jax
import jax.numpy as jnp
from jax import lax
from jax.sharding import PartitionSpec as P

BLOCK = 96
NS_STEPS = 8
CLU_DEV = 1


def newton_schulz(matrices):
    frob_norm = jnp.sqrt(jnp.sum(matrices * matrices, axis=(-2, -1), keepdims=True) + 1e-06)
    value = matrices / frob_norm
    for iteration in range(NS_STEPS):
        square = jnp.einsum("...ij,...kj->...ik", value, value, precision=lax.Precision.HIGHEST)
        value = 1.5 * value - 0.5 * jnp.einsum(
            "...ik,...kj->...ij", square, value, precision=lax.Precision.HIGHEST
        )
    return value


def block_gram(left, right):
    experts, units, width = left.shape
    nblocks = units // BLOCK
    lead_rows = left.reshape(experts, nblocks, BLOCK, width)
    member_rows = right.reshape(experts, nblocks, BLOCK, width)
    gram = jnp.einsum("nbid,nbjd->nibj", lead_rows, member_rows, preferred_element_type=jnp.float32)
    return gram.reshape(experts, BLOCK, units)


def polar_factors(gram):
    experts, height, units = gram.shape
    nblocks = units // BLOCK
    matrices = gram.reshape(experts, BLOCK, nblocks, BLOCK).transpose(0, 2, 1, 3)
    polar = newton_schulz(matrices).astype(jnp.bfloat16)
    return polar.transpose(0, 2, 1, 3).reshape(experts, BLOCK, units)


def align_rows(factors, slab, scale):
    experts, units, width = slab.shape
    nblocks = units // BLOCK
    turn = factors.reshape(experts, BLOCK, nblocks, BLOCK)
    member_rows = slab.reshape(experts, nblocks, BLOCK, width)
    turned = jnp.einsum("nibj,nbjd->nbid", turn, member_rows, preferred_element_type=jnp.float32)
    turned = turned * scale[:, None, None, None]
    return turned.reshape(experts, units, width).astype(jnp.bfloat16)


def on_device(w_up, cluster, counts):
    cluster_ids = cluster[:, 0]
    experts = cluster_ids.shape[0]
    clusters = CLU_DEV * lax.axis_size("expert")
    index = jnp.arange(experts, dtype=jnp.int32)
    labels = jnp.arange(clusters, dtype=jnp.int32)
    member = cluster_ids[None, :] == labels[:, None]
    score = counts * experts + (experts - 1 - index)
    best = jnp.max(jnp.where(member, score[None, :], -1), axis=1)
    leader = experts - 1 - best % experts
    anchor_of = jnp.sum(jnp.where(member, leader[:, None], 0), axis=0)
    total = jnp.sum(jnp.where(member, counts[None, :], 0), axis=1).astype(jnp.float32)
    weight = counts.astype(jnp.float32) / jnp.sum(jnp.where(member, total[:, None], 0.0), axis=0)
    columns = lax.all_to_all(w_up, "expert", split_axis=2, concat_axis=0, tiled=True)
    anchors = jnp.take(columns, anchor_of, axis=0)
    gram = lax.psum_scatter(block_gram(anchors, columns), "expert", scatter_dimension=0, tiled=True)
    polar = polar_factors(gram)
    aligned = align_rows(lax.all_gather(polar, "expert", axis=0, tiled=True), columns, weight)
    select = member.astype(jnp.bfloat16)
    summed = jnp.dot(select, aligned.reshape(experts, -1), preferred_element_type=jnp.float32)
    merged = summed.reshape(clusters, aligned.shape[1], aligned.shape[2]).astype(jnp.bfloat16)
    return lax.all_to_all(
        lax.all_to_all(merged, "expert", split_axis=0, concat_axis=2, tiled=True),
        "unit",
        split_axis=2,
        concat_axis=1,
        tiled=True,
    )


def solution(mesh):
    return jax.shard_map(
        on_device,
        mesh=mesh,
        in_specs=(P("expert", "unit", None), P(), P()),
        out_specs=P("expert", None, "unit"),
        check_vma=False,
    )
```

profile of v0, /device:TPU:1, one launch (start us, length us, event | category | flops | bytes accessed | tf_op | source)
XLA Modules:
  0.0 799.8 jit_solution(10294570698834870266)
XLA Ops:
  6.5 13.1 %copy.44 = bf16[4,192,4096]{1,0,2:T(4,128)(2,1)} copy(bf16[4,192,4096]{2,1,0:T(8,128)(2,1)} %param.3) | data formatting | bytes 12582912 | tf_op args[0]
  19.6 12.3 %all-to-all-start = ((bf16[4,192,4096]{1,0,2:T(4,128)(2,1)}), bf16[4,192,4096]{1,0,2:T(4,128)(2,1)}, u32[]{:S(2)}, u32[]{:S(2)}) async-start(bf16[4,192,4096]{1,0,2:T(4,128)(2,1)} %copy.44), calls=%async_computation | async-start | bytes 16777216 | tf_op jit(solution)/shard_map/all_to_all | solution.py:62
  32.3 187.8 %all-to-all-done = bf16[4,192,4096]{1,0,2:T(4,128)(2,1)} async-done(((bf16[4,192,4096]{1,0,2:T(4,128)(2,1)}), bf16[4,192,4096]{1,0,2:T(4,128)(2,1)}, u32[]{:S(2)}, u32[]{:S(2)}) %all-to-all-start) | async-done | bytes 6291488 | tf_op jit(solution)/shard_map/all_to_all | solution.py:62
  220.1 13.2 %copy.45 = bf16[4,192,32,128]{3,1,0,2:T(8,128)(2,1)} copy(bf16[4,192,32,128]{1,0,3,2:T(4,128)(2,1)} %bitcast.2) | data formatting | bytes 12582912 | tf_op jit(solution)/shard_map/all_to_all | solution.py:62
  233.3 6.7 gather_fusion
  240.0 13.4 %fusion.3 = f32[128,96,2,96]{3,1,2,0:T(8,128)} fusion(bf16[128,2,96,128]{3,2,1,0:T(8,128)(2,1)} %bitcast.128, bf16[128,2,96,128]{3,2,1,0:T(8,128)(2,1)} %bitcast.134, pred[128]{0:T(512)(128)(4,1)S(1)} %compare_and_fusion), kind=kOutput, calls=%fused_computation.6 | convolution fusion | flops 607125504 | bytes 22020224 | tf_op jit(solution)/shard_map/nbid,nbjd->nibj/dot_general | solution.py:27
  253.5 11.7 %copy.46 = f32[128,96,2,96]{0,3,2,1:T(8,128)} copy(f32[128,96,2,96]{3,1,2,0:T(8,128)} %fusion.3) | data formatting | bytes 18874368 | tf_op jit(solution)/shard_map/nbid,nbjd->nibj/transpose | solution.py:27
  265.2 12.7 %copy.47 = f32[128,96,192]{2,1,0:T(8,128)} copy(f32[128,96,192]{0,2,1:T(8,128)} %bitcast.130) | data formatting | bytes 18874368 | tf_op jit(solution)/shard_map/reshape | solution.py:28
  277.9 0.2 all-gather.2.cloned.1.call-start
  278.1 237.5 %reduce-scatter.2.cloned.1.call-done = f32[4,96,192]{2,1,0:T(8,128)} async-done(((f32[128,96,192]{2,1,0:T(8,128)}), f32[4,96,192]{2,1,0:T(8,128)}) %reduce-scatter.2.cloned.1.call-update) | async-done | bytes 294928 | tf_op jit(solution)/shard_map/reduce_scatter | solution.py:64
  515.6 1.2 copy.48
  516.8 0.2 copy.49
  517.1 1.0 fusion.18
  518.1 0.6 fusion.20
  518.7 0.9 fusion.36
  519.6 0.5 convolution_multiply_fusion.6
  520.2 0.9 fusion.34
  521.1 0.6 multiply_subtract_fusion.4
  521.7 0.9 fusion.37
  522.6 0.5 convolution_multiply_fusion.4
  523.1 0.9 fusion.35
  524.0 0.6 multiply_subtract_fusion.2
  524.6 0.9 fusion.38
  525.5 0.5 convolution_multiply_fusion.2
  526.0 0.9 fusion.33
  527.0 0.5 convolution_multiply_fusion.1
  527.5 1.0 fusion.21
  528.5 0.8 fusion.9
  529.4 0.8 copy.51
  530.4 90.1 %all-gather.2.cloned.1.call-done = bf16[128,96,192]{2,1,0:T(8,128)(2,1)} async-done(((bf16[4,96,192]{2,1,0:T(8,128)(2,1)}), bf16[128,96,192]{2,1,0:T(8,128)(2,1)}) %all-gather.2.cloned.1.call-update) | async-done | bytes 4718608 | tf_op jit(solution)/shard_map/all_gather | solution.py:66
  620.5 8.8 %copy.52 = bf16[128,96,192]{0,2,1:T(8,128)(2,1)} copy(bf16[128,96,192]{2,1,0:T(8,128)(2,1)} %all-gather.2.cloned.1.call-done) | data formatting | bytes 9437184 | tf_op jit(solution)/shard_map/all_gather | solution.py:66
  629.2 8.5 %copy.53 = bf16[128,96,2,96]{3,1,2,0:T(8,128)(2,1)} copy(bf16[128,96,2,96]{0,3,2,1:T(8,128)(2,1)} %bitcast.135) | data formatting | bytes 9437184 | tf_op jit(solution)/shard_map/reshape | solution.py:42
  637.7 6.4 multiply_convert_fusion
  644.1 8.0 %copy.65 = bf16[16,8,192,128]{3,1,2,0:T(8,128)(2,1)} copy(bf16[16,8,192,128]{3,2,1,0:T(8,128)(2,1)S(1)} %bitcast.133) | data formatting | bytes 12582912
  652.2 8.6 %copy.54 = bf16[24576,128]{1,0:T(8,128)(2,1)} copy(bf16[24576,128]{0,1:T(8,128)(2,1)} %bitcast.131) | data formatting | bytes 12582912 | tf_op jit(solution)/shard_map/dot_general | solution.py:68
  660.8 4.9 convolution_convert_fusion
  665.7 0.6 copy.55
  666.4 41.9 %all_to_all.54 = bf16[32,192,128]{2,1,0:T(8,128)(2,1)} all-to-all(bf16[32,192,128]{2,1,0:T(8,128)(2,1)S(1)} %copy.55), channel_id=1, replica_groups=mesh['expert'=32,'unit'=8] {'expert'}, dimensions={0} | all-to-all | bytes 3145728 | tf_op jit(solution)/shard_map/all_to_all | solution.py:71
  708.3 3.1 copy.60
  711.4 6.2 reshape.84
  717.6 0.5 broadcast.142
  718.1 23.6 %reduce.1 = bf16[4096,192]{1,0:T(8,128)(2,1)S(1)} reduce(bf16[4096,1,192]{2,1,0:T(2,128)(2,1)} %bitcast.136, bf16[]{:T(256)} %broadcast.142), dimensions={1}, to_apply=%bitcast.99.reduce_sub_computation | reduce | bytes 3145730
  741.8 4.4 reshape.85
  746.1 29.5 %all_to_all.55 = bf16[8,2,49152]{2,1,0:T(2,128)(2,1)S(1)} all-to-all(bf16[8,2,49152]{2,1,0:T(2,128)(2,1)} %reshape.85), channel_id=1, replica_groups=mesh['expert'=32,'unit'=8] {'unit'}, dimensions={0} | all-to-all | bytes 3145728 | tf_op jit(solution)/shard_map/all_to_all | solution.py:70
  775.7 4.9 reshape.86
  780.6 9.9 %copy.58 = bf16[1,192,4096]{2,1,0:T(8,128)(2,1)S(1)} copy(bf16[1,192,4096]{1,0,2:T(2,128)(2,1)} %bitcast.137) | data formatting | bytes 3145728 | tf_op jit(solution)/shard_map/all_to_all | solution.py:70
  790.5 0.6 copy.63
  791.3 1.6 copy.59
  (21 shorter events, 0.8 us)
Async XLA Ops:
  19.6 12.3 %copy-start.1 = (s32[128]{0:T(128)S(1)}, s32[128]{0:T(128)}, u32[]{:S(2)}) copy-start(s32[128]{0:T(128)} %param.5) | copy-start | bytes 1540
  19.6 12.4 %copy-start = (s32[128,1]{0,1:T(1,128)S(1)}, s32[128,1]{0,1:T(1,128)}, u32[]{:S(2)}) copy-start(s32[128,1]{0,1:T(1,128)} %param.4) | copy-start | bytes 1540
  19.6 200.5 %all-to-all-start = ((bf16[4,192,4096]{1,0,2:T(4,128)(2,1)}), bf16[4,192,4096]{1,0,2:T(4,128)(2,1)}, u32[]{:S(2)}, u32[]{:S(2)}) async-start(bf16[4,192,4096]{1,0,2:T(4,128)(2,1)} %copy.44), calls=%async_computation | async-start | bytes 16777216 | tf_op jit(solution)/shard_map/all_to_all | solution.py:62
  31.9 483.7 %reduce-scatter.2.cloned.1.call-start = ((), (), s32[]{:S(2)}) async-start(), calls=%async_computation.4 | async-start | bytes 12976128 | tf_op jit(solution)/shard_map/reduce_scatter | solution.py:64
  277.9 342.6 %all-gather.2.cloned.1.call-start = ((), (), s32[]{:S(2)}) async-start(), calls=%async_computation.5 | async-start | bytes 6488064 | tf_op jit(solution)/shard_map/all_gather | solution.py:66
Sparse Core Ops, SparseCore 0:
  278.0 237.5 reduce-scatter.1
  530.4 90.0 all-gather.1
where the time goes:
time: 802 us; the launch traced here: 800 us
  waiting for transfers between devices  515 us (64%)
  local copies, waits for them, and re-layouts  126 us (16%)
  blocking collectives  71.4 us (9%)
  matrix products  36.8 us (5%)
  other arithmetic  24.2 us (3%)
  between operations  13.7 us (2%)
  starting transfers between devices  12.5 us (2%)
    reduce_scatter x1, waiting for transfers between devices, on_device(): lax.psum_scatter(block_gram(anchors, columns), 'expert', scatter_dimensio...  237 us
    all_to_all x1, waiting for transfers between devices, on_device(): lax.all_to_all(w_up, 'expert', split_axis=2, concat_axis=0, tiled=True)  188 us
    all_gather x1, waiting for transfers between devices, on_device(): lax.all_gather(polar, 'expert', axis=0, tiled=True)  90.1 us
    all_to_all x1, blocking collectives, on_device(): lax.all_to_all(merged, 'expert', split_axis=0, concat_axis=2, tiled=True)  41.9 us
    unnamed x10, local copies, waits for them, and re-layouts  31.6 us
    all_to_all x1, blocking collectives, on_device(): lax.all_to_all(lax.all_to_all(merged, 'expert', split_axis=0, concat_axis...  29.5 us
    unnamed x1, other arithmetic  23.6 us
  transfers between devices with their start and end apart: 3, of which 3 were waited for; matrix products, arithmetic and copies ran while one was open for 0% of the time, Pallas kernels for 0%

commit v1 on v0

--- a/solution.py
+++ b/solution.py
@@ -6,6 +6,11 @@
 BLOCK = 96
 NS_STEPS = 8
 CLU_DEV = 1
+
+
+def exchange_gather(array, axis, dim):
+    repeated = jnp.stack([array] * lax.axis_size(axis))
+    return jnp.concatenate(lax.all_to_all(repeated, axis, 0, 0), axis=dim)
 
 
 def newton_schulz(matrices):
@@ -63,7 +68,7 @@
     anchors = jnp.take(columns, anchor_of, axis=0)
     gram = lax.psum_scatter(block_gram(anchors, columns), "expert", scatter_dimension=0, tiled=True)
     polar = polar_factors(gram)
-    aligned = align_rows(lax.all_gather(polar, "expert", axis=0, tiled=True), columns, weight)
+    aligned = align_rows(exchange_gather(polar, "expert", 0), columns, weight)
     select = member.astype(jnp.bfloat16)
     summed = jnp.dot(select, aligned.reshape(experts, -1), preferred_element_type=jnp.float32)
     merged = summed.reshape(clusters, aligned.shape[1], aligned.shape[2]).astype(jnp.bfloat16)

time: 802 us -> 849 us (1.059)
  waiting for transfers between devices: 515 us -> 564 us
  local copies, waits for them, and re-layouts: 126 us -> 115 us
    all_to_all x0 -> x1, waiting for transfers between devices: none -> 138 us  [exchange_gather(): return jnp.concatenate(lax.all_to_all(repeated, axis, 0, 0), axis=dim)]
    all_gather x1 -> x0, waiting for transfers between devices: 90.1 us -> none  [on_device(): lax.all_gather(polar, 'expert', axis=0, tiled=True)]
    reshape x2 -> x0, local copies, waits for them, and re-layouts: 9.31 us -> none  [the longest x1 8.49 us: align_rows(): turn = factors.reshape(experts, BLOCK, nblocks, BLOCK)]
    all_gather x1 -> x0, local copies, waits for them, and re-layouts: 8.78 us -> none  [on_device(): lax.all_gather(polar, 'expert', axis=0, tiled=True)]
where the time goes in v1:
time: 849 us; the launch traced here: 847 us
  waiting for transfers between devices  564 us (66%)
  local copies, waits for them, and re-layouts  115 us (14%)
  blocking collectives  71.2 us (8%)
  matrix products  40.8 us (5%)
  other arithmetic  24.2 us (3%)
  starting transfers between devices  19.2 us (2%)
  between operations  13.6 us (2%)
    reduce_scatter x1, waiting for transfers between devices, on_device(): lax.psum_scatter(block_gram(anchors, columns), 'expert', scatter_dimensio...  238 us
    all_to_all x1, waiting for transfers between devices, on_device(): lax.all_to_all(w_up, 'expert', split_axis=2, concat_axis=0, tiled=True)  188 us
    all_to_all x1, waiting for transfers between devices, exchange_gather(): return jnp.concatenate(lax.all_to_all(repeated, axis, 0, 0), axis=dim)  138 us
    all_to_all x1, blocking collectives, on_device(): lax.all_to_all(merged, 'expert', split_axis=0, concat_axis=2, tiled=True)  41 us
    unnamed x10, local copies, waits for them, and re-layouts  34.3 us
    all_to_all x1, blocking collectives, on_device(): lax.all_to_all(lax.all_to_all(merged, 'expert', split_axis=0, concat_axis...  30.2 us
    unnamed x1, other arithmetic  23.6 us
  transfers between devices with their start and end apart: 3, of which 3 were waited for; matrix products, arithmetic and copies ran while one was open for 0% of the time, Pallas kernels for 0%

profile of v1, /device:TPU:1, one launch (start us, length us, event | category | flops | bytes accessed | tf_op | source)
XLA Modules:
  0.0 847.2 jit_solution(5308956048008398351)
XLA Ops:
  6.5 13.1 %copy.39 = bf16[4,192,4096]{1,0,2:T(4,128)(2,1)} copy(bf16[4,192,4096]{2,1,0:T(8,128)(2,1)} %param.3) | data formatting | bytes 12582912 | tf_op args[0]
  19.6 12.3 %all-to-all-start = ((bf16[4,192,4096]{1,0,2:T(4,128)(2,1)}), bf16[4,192,4096]{1,0,2:T(4,128)(2,1)}, u32[]{:S(2)}, u32[]{:S(2)}) async-start(bf16[4,192,4096]{1,0,2:T(4,128)(2,1)} %copy.39), calls=%async_computation | async-start | bytes 16777216 | tf_op jit(solution)/shard_map/all_to_all | solution.py:67
  32.3 187.8 %all-to-all-done = bf16[4,192,4096]{1,0,2:T(4,128)(2,1)} async-done(((bf16[4,192,4096]{1,0,2:T(4,128)(2,1)}), bf16[4,192,4096]{1,0,2:T(4,128)(2,1)}, u32[]{:S(2)}, u32[]{:S(2)}) %all-to-all-start) | async-done | bytes 6291488 | tf_op jit(solution)/shard_map/all_to_all | solution.py:67
  220.1 13.2 %copy.40 = bf16[4,192,32,128]{3,1,0,2:T(8,128)(2,1)} copy(bf16[4,192,32,128]{1,0,3,2:T(4,128)(2,1)} %bitcast.2) | data formatting | bytes 12582912 | tf_op jit(solution)/shard_map/all_to_all | solution.py:67
  233.3 6.7 gather_fusion
  240.0 13.4 %fusion.3 = f32[128,96,2,96]{3,1,2,0:T(8,128)} fusion(bf16[128,2,96,128]{3,2,1,0:T(8,128)(2,1)} %bitcast.128, bf16[128,2,96,128]{3,2,1,0:T(8,128)(2,1)} %bitcast.134, pred[128]{0:T(512)(128)(4,1)S(1)} %compare_and_fusion), kind=kOutput, calls=%fused_computation.6 | convolution fusion | flops 607125504 | bytes 22020224 | tf_op jit(solution)/shard_map/nbid,nbjd->nibj/dot_general | solution.py:32
  253.5 11.7 %copy.41 = f32[128,96,2,96]{0,3,2,1:T(8,128)} copy(f32[128,96,2,96]{3,1,2,0:T(8,128)} %fusion.3) | data formatting | bytes 18874368 | tf_op jit(solution)/shard_map/nbid,nbjd->nibj/transpose | solution.py:32
  265.2 12.7 %copy.42 = f32[128,96,192]{2,1,0:T(8,128)} copy(f32[128,96,192]{0,2,1:T(8,128)} %bitcast.130) | data formatting | bytes 18874368 | tf_op jit(solution)/shard_map/reshape | solution.py:33
  277.9 237.7 %reduce-scatter.2.cloned.1.call-done = f32[4,96,192]{2,1,0:T(8,128)} async-done(((f32[128,96,192]{2,1,0:T(8,128)}), f32[4,96,192]{2,1,0:T(8,128)}) %reduce-scatter.2.cloned.1.call-update) | async-done | bytes 294928 | tf_op jit(solution)/shard_map/reduce_scatter | solution.py:69
  515.6 1.2 copy.43
  516.8 0.2 copy.44
  517.0 0.1 multiply_reduce_fusion
  517.1 1.0 fusion.18
  518.1 0.6 fusion.20
  518.7 0.9 fusion.36
  519.6 0.5 convolution_multiply_fusion.6
  520.2 0.9 fusion.34
  521.1 0.6 multiply_subtract_fusion.4
  521.7 0.9 fusion.37
  522.6 0.5 convolution_multiply_fusion.4
  523.1 0.9 fusion.35
  524.0 0.6 multiply_subtract_fusion.2
  524.6 0.9 fusion.38
  525.5 0.5 convolution_multiply_fusion.2
  526.0 0.9 fusion.33
  527.0 0.5 convolution_multiply_fusion.1
  527.5 1.0 fusion.21
  528.5 0.8 fusion.9
  529.3 0.1 copy.45
  529.4 4.2 stack.3
  533.6 6.8 all-to-all-start.1
  540.6 138.1 %all-to-all-done.1 = bf16[32,4,96,192]{2,3,1,0:T(8,128)(2,1)} async-done(((bf16[32,4,96,192]{2,3,1,0:T(8,128)(2,1)}), bf16[32,4,96,192]{2,3,1,0:T(8,128)(2,1)}, u32[]{:S(2)}, u32[]{:S(2)}) %all-to-all-start.1) | async-done | bytes 4718624 | tf_op jit(solution)/shard_map/all_to_all | solution.py:13
  678.7 10.4 %multiply_convert_fusion = bf16[128,2,96,128]{3,2,1,0:T(8,128)(2,1)} fusion(f32[128]{0:T(128)S(1)} %convert_divide_fusion, bf16[128,96,2,96]{1,3,2,0:T(8,128)(2,1)} %bitcast.22, bf16[128,2,96,128]{3,2,1,0:T(8,128)(2,1)} %bitcast.129), kind=kOutput, calls=%fused_computation.1 | convolution fusion | flops 610271232 | bytes 17302016 | tf_op jit(solution)/shard_map/nibj,nbjd->nbid/dot_general | solution.py:49
  689.1 10.7 %copy.59 = bf16[16,8,192,128]{3,1,2,0:T(8,128)(2,1)} copy(bf16[16,8,192,128]{3,2,1,0:T(8,128)(2,1)} %bitcast.133) | data formatting | bytes 12582912
  699.8 8.6 %copy.47 = bf16[24576,128]{1,0:T(8,128)(2,1)} copy(bf16[24576,128]{0,1:T(8,128)(2,1)} %bitcast.131) | data formatting | bytes 12582912 | tf_op jit(solution)/shard_map/dot_general | solution.py:73
  708.4 5.0 convolution_convert_fusion
  713.4 0.6 copy.48
  714.0 41.0 %all_to_all.59 = bf16[32,192,128]{2,1,0:T(8,128)(2,1)} all-to-all(bf16[32,192,128]{2,1,0:T(8,128)(2,1)S(1)} %copy.48), channel_id=1, replica_groups=mesh['expert'=32,'unit'=8] {'expert'}, dimensions={0} | all-to-all | bytes 3145728 | tf_op jit(solution)/shard_map/all_to_all | solution.py:76
  755.0 3.1 copy.54
  758.2 6.2 reshape.78
  764.4 0.5 broadcast.143
  764.9 23.6 %reduce.1 = bf16[4096,192]{1,0:T(8,128)(2,1)S(1)} reduce(bf16[4096,1,192]{2,1,0:T(2,128)(2,1)} %bitcast.135, bf16[]{:T(256)} %broadcast.143), dimensions={1}, to_apply=%bitcast.99.reduce_sub_computation | reduce | bytes 3145730
  788.5 4.4 reshape.79
  792.9 30.2 %all_to_all.60 = bf16[8,2,49152]{2,1,0:T(2,128)(2,1)S(1)} all-to-all(bf16[8,2,49152]{2,1,0:T(2,128)(2,1)} %reshape.79), channel_id=1, replica_groups=mesh['expert'=32,'unit'=8] {'unit'}, dimensions={0} | all-to-all | bytes 3145728 | tf_op jit(solution)/shard_map/all_to_all | solution.py:75
  823.1 4.9 reshape.80
  828.0 9.9 %copy.51 = bf16[1,192,4096]{2,1,0:T(8,128)(2,1)S(1)} copy(bf16[1,192,4096]{1,0,2:T(2,128)(2,1)} %bitcast.136) | data formatting | bytes 3145728 | tf_op jit(solution)/shard_map/all_to_all | solution.py:75
  837.9 0.6 copy.57
  838.7 1.6 copy.52
  (18 shorter events, 0.5 us)
Async XLA Ops:
  19.6 12.3 %copy-start.1 = (s32[128]{0:T(128)S(1)}, s32[128]{0:T(128)}, u32[]{:S(2)}) copy-start(s32[128]{0:T(128)} %param.5) | copy-start | bytes 1540
  19.6 12.4 %copy-start = (s32[128,1]{0,1:T(1,128)S(1)}, s32[128,1]{0,1:T(1,128)}, u32[]{:S(2)}) copy-start(s32[128,1]{0,1:T(1,128)} %param.4) | copy-start | bytes 1540
  19.6 200.5 %all-to-all-start = ((bf16[4,192,4096]{1,0,2:T(4,128)(2,1)}), bf16[4,192,4096]{1,0,2:T(4,128)(2,1)}, u32[]{:S(2)}, u32[]{:S(2)}) async-start(bf16[4,192,4096]{1,0,2:T(4,128)(2,1)} %copy.39), calls=%async_computation | async-start | bytes 16777216 | tf_op jit(solution)/shard_map/all_to_all | solution.py:67
  31.9 483.7 %reduce-scatter.2.cloned.1.call-start = ((), (), s32[]{:S(2)}) async-start(), calls=%async_computation.5 | async-start | bytes 12976128 | tf_op jit(solution)/shard_map/reduce_scatter | solution.py:69
  533.6 145.1 %all-to-all-start.1 = ((bf16[32,4,96,192]{2,3,1,0:T(8,128)(2,1)}), bf16[32,4,96,192]{2,3,1,0:T(8,128)(2,1)}, u32[]{:S(2)}, u32[]{:S(2)}) async-start(bf16[32,4,96,192]{2,3,1,0:T(8,128)(2,1)} %stack.3), calls=%async_computation.2 | async-start | bytes 12582912 | tf_op jit(solution)/shard_map/all_to_all | solution.py:13
Sparse Core Ops, SparseCore 0:
  278.0 237.5 reduce-scatter.1
